TPU v7x, 32 devices: a whole 2x2x4 slice. The times are simulated.
32 devices in a mesh: group: 1, wide: 32 (over z, y, x, core).
Axes of the slice: x: 2, y: 2, z: 4, core: 2. Of those that a mesh axis runs over, the one named last changes fastest.
Arguments:
- ssd_x: bfloat16 [2048, 4096], P(('group', 'wide')), may hold values from -6 to 6
- ssd_z: bfloat16 [2048, 4096], P(('group', 'wide')), may hold values from -6 to 6
- ssd_b: bfloat16 [2048, 128], P(('group', 'wide')), may hold values from -2 to 2
- ssd_c: bfloat16 [2048, 128], P(('group', 'wide')), may hold values from -2 to 2
- dt_raw: bfloat16 [2048, 64], P(('group', 'wide')), may hold values from -4 to 4
- dt_bias: float32 [64], replicated, may hold values from -4 to -1
- a_log: float32 [64], replicated, may hold values from -1.5 to 1.5
- d_skip: float32 [64], replicated, may hold values from 0.5 to 1.5
- norm_gain: float32 [4096], replicated, may hold values from 0.1 to 1.9
- cache_state: bfloat16 [64, 64, 64, 128], P(('group', 'wide')), may hold values from -2 to 2
- cache_owner: int32 [64], P('group'), may hold values from 0 to 63
- resid: bfloat16 [2048, 2048], P(('group', 'wide')), may hold values from -3 to 3
- w_out: bfloat16 [4096, 2048], P('wide'), may hold values from -0.09375 to 0.09375
- moe_gain: float32 [2048], replicated, may hold values from 0.1 to 1.9
- expert_ids: int32 [2048, 10], P(('group', 'wide')), may hold values from 0 to 31, all different within a row; in each aligned block of 64 rows (0 to 63, 64 to 127, ...) at most 32 rows name the same one
- route_weight: int32 [2048, 10], P(('group', 'wide')), may hold values from 1 to 1023
- expert_home: int32 [32], replicated, may hold values from 0 to 31, each once
- w_gate: bfloat16 [32, 2048, 384], P('wide'), may hold values from -0.125 to 0.125
- w_up: bfloat16 [32, 2048, 384], P('wide'), may hold values from -0.125 to 0.125
- w_down: bfloat16 [32, 384, 2048], P('wide'), may hold values from -0.3125 to 0.3125
Outputs:
- ssd_out: bfloat16 [2048, 4096], P(('group', 'wide'))
- moe_out: bfloat16 [2048, 2048], P(('group', 'wide'))
Inputs may be any that keep to these rules, and one draw needn't show every extreme that they name: `cache_owner`: slot s of cache_state holds a cached prefix state; several requests may continue from the same slot. `expert_ids`: each token names 10 different experts. In each aligned block of 64 tokens (the tokens of one device) no expert is named by more than 32 tokens, and in every draw some expert is named by exactly 32 tokens of some block. `expert_home`: A permutation of the experts.
All inputs are finite; a program needn't handle non-finite values.
Results may differ from a plain program's by a relative error of at most 0.02.
Values may be sent and summed in bfloat16 or wider, within the bound.
No kernel may reach another device: no remote copies, remote signals or barrier semaphores. Data moves between devices by JAX's collectives and lax.ppermute only.
A program may use at most 128 MiB of HBM per device.

v0:
```python
import jax
import jax.numpy as jnp
from jax import lax
from jax.sharding import PartitionSpec as P

SEQ = 32


def intra_terms(inputs, step_size, cumulative, b_proj, c_proj, skip_gain):
    scores = jnp.einsum("rtn,rsn->rts", c_proj, b_proj, preferred_element_type=jnp.float32)
    length = inputs.shape[1]
    causal = jnp.arange(length)[:, None] >= jnp.arange(length)[None, :]
    cum_heads = jnp.swapaxes(cumulative, 1, 2)
    log_gap = cum_heads[..., :, None] - cum_heads[..., None, :]
    decays = jnp.where(causal, jnp.exp(jnp.where(causal, log_gap, 0.0)), 0.0)
    mixing = (scores[:, None] * decays * jnp.swapaxes(step_size, 1, 2)[:, :, None, :]).astype(
        jnp.bfloat16
    )
    result = jnp.einsum("rhts,rshp->rthp", mixing, inputs, preferred_element_type=jnp.float32)
    result = result + skip_gain[None, None, :, None] * inputs.astype(jnp.float32)
    return result.astype(jnp.bfloat16)


def state_terms(c_proj, cumulative, start_state):
    product = jnp.einsum("rtn,rhpn->rthp", c_proj, start_state, preferred_element_type=jnp.float32)
    return (product * jnp.exp(cumulative)[..., None]).astype(jnp.bfloat16)


def expert_mlp(row_set, gate_weight, up_weight, down_weight):
    gate_out = jnp.dot(row_set, gate_weight, preferred_element_type=jnp.float32)
    up_out = jnp.dot(row_set, up_weight, preferred_element_type=jnp.float32)
    hidden = (jax.nn.silu(gate_out) * up_out).astype(jnp.bfloat16)
    return jnp.dot(hidden, down_weight, preferred_element_type=jnp.float32).astype(jnp.bfloat16)


def head_steps(raw_steps, bias_part, rate_part, requests):
    step_size = jax.nn.softplus(raw_steps.astype(jnp.float32) + bias_part)
    step_size = step_size.reshape(requests, SEQ, step_size.shape[-1])
    return (step_size, jnp.cumsum(step_size * rate_part, axis=1))


def local(
    ssd_x,
    ssd_z,
    ssd_b,
    ssd_c,
    dt_raw,
    dt_bias,
    a_log,
    d_skip,
    norm_gain,
    cache_state,
    cache_owner,
    resid,
    w_out,
    moe_gain,
    expert_ids,
    route_weight,
    expert_home,
    w_gate,
    w_up,
    w_down,
):
    devices = lax.axis_size("wide")
    my_index = lax.axis_index("wide")
    tok_dev = ssd_x.shape[0]
    heads_all = dt_raw.shape[1]
    per_dev = heads_all // devices
    head_dim = ssd_x.shape[1] // heads_all
    state_size = ssd_b.shape[1]
    req_local = tok_dev // SEQ
    rates = -jnp.exp(a_log)
    bias_part = lax.dynamic_slice_in_dim(dt_bias, my_index * per_dev, per_dev)
    rate_part = lax.dynamic_slice_in_dim(rates, my_index * per_dev, per_dev)
    by_heads = lax.all_to_all(cache_state, "wide", split_axis=1, concat_axis=0, tiled=True)
    start_state = jnp.take(by_heads, cache_owner, axis=0)
    requests = cache_owner.shape[0]
    tokens_all = requests * SEQ
    local_step, local_cum = head_steps(dt_raw, dt_bias, rates, req_local)
    intra = intra_terms(
        ssd_x.reshape(req_local, SEQ, heads_all, head_dim),
        local_step,
        local_cum,
        ssd_b.reshape(req_local, SEQ, state_size),
        ssd_c.reshape(req_local, SEQ, state_size),
        d_skip,
    )
    intra = intra.reshape(tok_dev, heads_all * head_dim)
    c_all = lax.all_gather(ssd_c, "wide", axis=0, tiled=True)
    head_raw = lax.all_to_all(dt_raw, "wide", split_axis=1, concat_axis=0, tiled=True)
    step_size, cumulative = head_steps(head_raw, bias_part, rate_part, requests)
    carried_head = state_terms(c_all.reshape(requests, SEQ, state_size), cumulative, start_state)
    carried = lax.all_to_all(
        carried_head.reshape(tokens_all, per_dev * head_dim),
        "wide",
        split_axis=0,
        concat_axis=1,
        tiled=True,
    )
    mixed = intra.astype(jnp.float32) + carried.astype(jnp.float32)
    gated = mixed * jax.nn.silu(ssd_z.astype(jnp.float32))
    ssd_out = (
        gated * lax.rsqrt(jnp.mean(gated * gated, axis=-1, keepdims=True) + 1e-05) * norm_gain
    ).astype(jnp.bfloat16)
    width = resid.shape[1]
    projected = jnp.dot(
        ssd_out,
        lax.all_gather(w_out, "wide", axis=0, tiled=True),
        preferred_element_type=jnp.float32,
    )
    topk = expert_ids.shape[1]
    expert_count = expert_home.shape[0]
    wide_moe = resid.astype(jnp.float32) + projected
    normed = (
        wide_moe
        * lax.rsqrt(jnp.mean(wide_moe * wide_moe, axis=-1, keepdims=True) + 1e-05)
        * moe_gain
    ).astype(jnp.bfloat16)
    weight_f = route_weight.astype(jnp.float32)
    share = weight_f / jnp.sum(weight_f, axis=-1, keepdims=True)
    lookup = expert_ids[..., None] == jnp.arange(expert_count, dtype=jnp.int32)
    target = jnp.sum(jnp.where(lookup, expert_home, 0), axis=-1)
    pair_count = tok_dev * topk
    flat_target = target.reshape(pair_count)
    one_hot = (flat_target[:, None] == jnp.arange(devices, dtype=jnp.int32)).astype(jnp.int32)
    before = jnp.cumsum(one_hot, axis=0) - one_hot
    slot_of = jnp.sum(before * one_hot, axis=-1)
    capacity = tok_dev * topk // expert_count * 8 // 5
    position = flat_target * capacity + slot_of
    source_row = (
        jnp.zeros((devices * capacity,), jnp.int32)
        .at[position]
        .set(jnp.arange(pair_count, dtype=jnp.int32) // topk + 1)
    )
    filled = source_row > 0
    fetched = jnp.take(normed, jnp.maximum(source_row - 1, 0), axis=0)
    send_rows = jnp.where(filled[:, None], fetched, jnp.zeros((), jnp.bfloat16)).reshape(
        devices, capacity, width
    )
    received = lax.all_to_all(send_rows, "wide", split_axis=0, concat_axis=0, tiled=True)
    flat_rows = received.reshape(-1, received.shape[-1])
    outputs = expert_mlp(flat_rows, w_gate[0], w_up[0], w_down[0]).reshape(received.shape)
    returned = lax.all_to_all(outputs, "wide", split_axis=0, concat_axis=0, tiled=True)
    gathered = jnp.take(returned.reshape(devices * capacity, width), position, axis=0).reshape(
        tok_dev, topk, width
    )
    moe_out = jnp.sum(gathered.astype(jnp.float32) * share[..., None], axis=1).astype(jnp.bfloat16)
    return (ssd_out, moe_out)


def solution(mesh):
    in_specs = (
        P(("group", "wide"), None),
        P(("group", "wide"), None),
        P(("group", "wide"), None),
        P(("group", "wide"), None),
        P(("group", "wide"), None),
        P(),
        P(),
        P(),
        P(),
        P(("group", "wide"), None, None, None),
        P("group"),
        P(("group", "wide"), None),
        P("wide", None),
        P(),
        P(("group", "wide"), None),
        P(("group", "wide"), None),
        P(),
        P("wide", None, None),
        P("wide", None, None),
        P("wide", None, None),
    )
    out_specs = (P(("group", "wide"), None), P(("group", "wide"), None))
    return jax.shard_map(local, mesh=mesh, in_specs=in_specs, out_specs=out_specs, check_vma=False)
```

profile of v0, /device:TPU:0, one launch (start us, length us, event | category | flops | bytes accessed | tf_op | source)
XLA Modules:
  0.0 430.2 jit_solution(291242435058443857)
XLA Ops:
  7.2 0.0 copy-start
  7.2 0.0 all-gather.2.cloned.1.call-start
  7.2 0.7 all-gather.2.cloned.1.call-update
  7.9 1.4 copy.108
  9.3 7.3 %all-to-all-start.1 = ((bf16[64,32,2]{0,2,1:T(2,128)(2,1)}), bf16[64,32,2]{0,2,1:T(2,128)(2,1)S(1)}, u32[]{:S(2)}, u32[]{:S(2)}) async-start(bf16[64,32,2]{0,2,1:T(2,128)(2,1)} %bitcast.14), calls=%async_computation.1 | async-start | bytes 32768 | tf_op jit(solution)/shard_map/all_to_all | solution.py:90
  16.7 3.1 copy.105
  19.8 3.9 all-to-all-done.1
  23.8 3.5 all-to-all-start
  27.3 0.1 select_reduce_fusion
  27.4 0.1 copy.115
  27.5 0.1 eq.42
  27.6 0.1 reshape.191
  27.8 0.1 dynamic_slice.7
  27.9 0.1 dynamic_slice.6
  28.0 0.1 reduce_window_sum.37
  28.1 0.1 copy.99
  28.2 0.1 copy.101
  28.2 1.1 reshape.189
  29.4 0.1 fusion.47
  29.5 1.9 fusion.12
  31.5 2.5 copy.104
  34.0 2.1 reshape.196
  36.2 1.5 reduce-window.6
  37.6 0.3 slice_reduce_fusion
  38.0 84.1 %all_gather.6 = bf16[2048,128]{1,0:T(8,128)(2,1)S(1)} all-gather(bf16[64,128]{1,0:T(8,128)(2,1)S(1)} %copy-done.6), channel_id=1, replica_groups=mesh['group'=1,'wide'=32] {'wide'}, dimensions={0}, use_global_device_ids=true | all-gather | bytes 540672 | tf_op jit(solution)/shard_map/all_gather | solution.py:89
  122.1 0.1 reshape.197
  122.1 0.1 copy.110
  122.2 0.1 fusion.33
  122.3 1.4 copy.111
  123.7 2.4 reduce-window_exponential_fusion
  126.1 1.9 copy.112
  128.0 3.2 copy.107
  131.1 3.8 gather_fusion
  134.9 3.7 fusion
  138.6 2.1 copy.113
  140.7 3.2 all_to_all.45
  143.9 15.3 %all-to-all-start.2 = ((bf16[32,64,128]{2,1,0:T(8,128)(2,1)}), bf16[32,64,128]{2,1,0:T(8,128)(2,1)S(1)}, u32[]{:S(2)}, u32[]{:S(2)}) async-start(bf16[32,64,128]{2,1,0:T(8,128)(2,1)} %all_to_all.45), calls=%async_computation.2 | async-start | bytes 1048576 | tf_op jit(solution)/shard_map/all_to_all | solution.py:93
  159.2 0.1 copy.120
  159.3 0.1 mul.161
  159.4 0.1 fusion.31
  159.6 4.1 scatter_custom_fusion
  163.7 0.1 broadcast_in_dim.101
  163.8 0.1 broadcast_in_dim.103
  163.9 10.9 %all-to-all-done.2 = bf16[32,64,128]{2,1,0:T(8,128)(2,1)S(1)} async-done(((bf16[32,64,128]{2,1,0:T(8,128)(2,1)}), bf16[32,64,128]{2,1,0:T(8,128)(2,1)S(1)}, u32[]{:S(2)}, u32[]{:S(2)}) %all-to-all-start.2) | async-done | bytes 524320 | tf_op jit(solution)/shard_map/all_to_all | solution.py:93
  174.8 1.5 multiply_reduce_fusion.1
  176.3 0.2 multiply_convert_fusion.3
  176.6 0.0 all-gather.2.cloned.1.call-done
  176.6 9.1 %multiply_reduce_fusion.2 = (f32[64]{0:T(128)S(1)}, f32[64,2048]{1,0:T(8,128)S(1)}) fusion(bf16[64,4096]{1,0:T(8,128)(2,1)S(1)} %multiply_convert_fusion.3, bf16[4096,2048]{1,0:T(8,128)(2,1)} %all-gather.2.cloned.1.call-done, bf16[64,2048]{1,0:T(8,128)(2,1)S(1)} %copy-done.4), kind=kOutput, calls=%fused_computation.42 | convolution fusion | flops 1074266112 | bytes 18088192 | tf_op jit(solution)/shard_map/dot_general | solution.py:106
  185.7 0.1 multiply_convert_fusion.4
  185.8 6.0 %gather_fusion.1 = bf16[1024,2048]{1,0:T(8,128)(2,1)} fusion(bf16[64,2048]{1,0:T(8,128)(2,1)S(1)} %multiply_convert_fusion.4, s32[1024]{0:T(1024)S(1)} %fusion.38), kind=kCustom, calls=%fused_computation.1 | custom fusion | bytes 8392704 | tf_op jit(solution)/shard_map/jit(_take)/gather | solution.py:136
  191.8 2.6 select_select_fusion
  194.4 96.4 %all_to_all.54 = bf16[32,32,2048]{2,1,0:T(8,128)(2,1)S(1)} all-to-all(bf16[32,32,2048]{2,1,0:T(8,128)(2,1)S(1)} %select_select_fusion), channel_id=1, replica_groups=mesh['group'=1,'wide'=32] {'wide'}, dimensions={0} | all-to-all | bytes 8388608 | tf_op jit(solution)/shard_map/all_to_all | solution.py:140
  290.8 2.0 copy-done.1
  292.8 3.6 fusion.8
  296.4 7.8 %convolution_convert_fusion = bf16[1024,2048]{1,0:T(8,128)(2,1)} fusion(bf16[1,384,2048]{2,1,0:T(8,128)(2,1)S(1)} %copy-done, f32[1024,384]{1,0:T(8,128)} %fusion.8, bf16[1024,2048]{1,0:T(8,128)(2,1)} %bitcast.90, bf16[1,2048,384]{2,1,0:T(8,128)(2,1)S(1)} %copy-done.15), kind=kOutput, calls=%fused_computation.6 | convolution fusion | flops 3225681920 | bytes 13107200 | tf_op jit(solution)/shard_map/dot_general | solution.py:33
  304.1 4.0 all-to-all-start.4
  308.2 0.1 reduce_sum.61
  308.3 0.1 copy.118
  308.4 0.1 copy.119
  308.6 0.1 copy.121
  308.7 93.2 %all-to-all-done.4 = bf16[32,32,2048]{2,1,0:T(8,128)(2,1)} async-done(((bf16[32,32,2048]{2,1,0:T(8,128)(2,1)}), bf16[32,32,2048]{2,1,0:T(8,128)(2,1)}, u32[]{:S(2)}, u32[]{:S(2)}) %all-to-all-start.4) | async-done | bytes 4194336 | tf_op jit(solution)/shard_map/all_to_all | solution.py:143
  401.9 9.7 %gather_fusion.2 = bf16[640,2048]{1,0:T(8,128)(2,1)} fusion(bf16[1024,2048]{1,0:T(8,128)(2,1)} %bitcast.24, s32[1024]{0:T(1024)S(1)} %pad_clamp_fusion), kind=kCustom, calls=%fused_computation.2 | custom fusion | bytes 5245440 | tf_op jit(solution)/shard_map/jit(_take)/gather | solution.py:144
  411.5 5.4 %gather.20 = bf16[64,10,2048]{2,1,0:T(8,128)(2,1)} reshape(bf16[640,2048]{1,0:T(8,128)(2,1)} %gather_fusion.2) | data formatting | bytes 5242880 | tf_op jit(solution)/shard_map/jit(_take)/gather | solution.py:144
  416.9 6.4 %multiply_reduce_fusion = bf16[64,2048]{1,0:T(8,128)(2,1)} fusion(f32[64,10]{1,0:T(8,128)S(1)} %copy.121, bf16[64,10,2048]{2,1,0:T(8,128)(2,1)} %gather.20, pred[64,10]{1,0:T(8,128)(4,1)S(1)} %copy.119), kind=kLoop, calls=%fused_computation.4 | loop fusion | flops 5111808 | bytes 2886784 | tf_op jit(solution)/shard_map/reduce_sum | solution.py:147
  (59 shorter events, 0.3 us)
Async XLA Ops:
  7.2 289.2 %copy-start = (bf16[1,384,2048]{2,1,0:T(8,128)(2,1)S(1)}, bf16[1,384,2048]{2,1,0:T(8,128)(2,1)}, u32[]{:S(2)}) copy-start(bf16[1,384,2048]{2,1,0:T(8,128)(2,1)} %param.39) | copy-start | bytes 4718596
  7.2 169.4 %all-gather.2.cloned.1.call-start = ((), (), s32[]{:S(2)}) async-start(), calls=%async_computation.5 | async-start | bytes 17301504 | tf_op jit(solution)/shard_map/all_gather | solution.py:108
  9.3 14.4 %all-to-all-start.1 = ((bf16[64,32,2]{0,2,1:T(2,128)(2,1)}), bf16[64,32,2]{0,2,1:T(2,128)(2,1)S(1)}, u32[]{:S(2)}, u32[]{:S(2)}) async-start(bf16[64,32,2]{0,2,1:T(2,128)(2,1)} %bitcast.14), calls=%async_computation.1 | async-start | bytes 32768 | tf_op jit(solution)/shard_map/all_to_all | solution.py:90
  19.8 7.5 %copy-start.11 = (s32[64,10]{0,1:T(8,128)S(1)}, s32[64,10]{0,1:T(8,128)}, u32[]{:S(2)}) copy-start(s32[64,10]{0,1:T(8,128)} %param.34) | copy-start | bytes 7684
  19.8 7.5 %copy-start.13 = (s32[32]{0:T(128)S(1)}, s32[32]{0:T(128)}, u32[]{:S(2)}) copy-start(s32[32]{0:T(128)} %param.36) | copy-start | bytes 388
  19.8 8.0 %copy-start.16 = (f32[64]{0:T(128)S(1)}, f32[64]{0:T(128)}, u32[]{:S(2)}) copy-start(f32[64]{0:T(128)} %param.26) | copy-start | bytes 772
  19.8 8.1 %copy-start.12 = (f32[64]{0:T(128)S(1)}, f32[64]{0:T(128)}, u32[]{:S(2)}) copy-start(f32[64]{0:T(128)} %param.25) | copy-start | bytes 772
  19.8 8.2 %copy-start.5 = (bf16[64,64]{1,0:T(8,128)(2,1)S(1)}, bf16[64,64]{1,0:T(8,128)(2,1)}, u32[]{:S(2)}) copy-start(bf16[64,64]{1,0:T(8,128)(2,1)} %param.24) | copy-start | bytes 24580
  19.8 8.4 %copy-start.3 = (bf16[64,4096]{1,0:T(8,128)(2,1)S(1)}, bf16[64,4096]{1,0:T(8,128)(2,1)}, u32[]{:S(2)}) copy-start(bf16[64,4096]{1,0:T(8,128)(2,1)} %param.20) | copy-start | bytes 1572868
  23.8 104.2 %all-to-all-start = ((bf16[2,64,64,128]{3,2,0,1:T(8,128)(2,1)}), bf16[2,64,64,128]{3,2,0,1:T(8,128)(2,1)}, u32[]{:S(2)}, u32[]{:S(2)}) async-start(bf16[2,64,64,128]{3,2,0,1:T(8,128)(2,1)} %copy.105), calls=%async_computation | async-start | bytes 4194304 | tf_op jit(solution)/shard_map/all_to_all | solution.py:75
  27.2 2.2 copy-start.6
  27.3 2.1 copy-start.9
  27.3 2.3 copy-start.17
  34.0 3.9 copy-start.18
  143.9 32.4 %copy-start.8 = (f32[4096]{0:T(1024)S(1)}, f32[4096]{0:T(1024)}, u32[]{:S(2)}) copy-start(f32[4096]{0:T(1024)} %param.28) | copy-start | bytes 49156
  143.9 30.9 %all-to-all-start.2 = ((bf16[32,64,128]{2,1,0:T(8,128)(2,1)}), bf16[32,64,128]{2,1,0:T(8,128)(2,1)S(1)}, u32[]{:S(2)}, u32[]{:S(2)}) async-start(bf16[32,64,128]{2,1,0:T(8,128)(2,1)} %all_to_all.45), calls=%async_computation.2 | async-start | bytes 1048576 | tf_op jit(solution)/shard_map/all_to_all | solution.py:93
  163.9 12.7 %copy-start.4 = (bf16[64,2048]{1,0:T(8,128)(2,1)S(1)}, bf16[64,2048]{1,0:T(8,128)(2,1)}, u32[]{:S(2)}) copy-start(bf16[64,2048]{1,0:T(8,128)(2,1)} %param.31) | copy-start | bytes 786436
  176.5 9.1 %copy-start.2 = (bf16[64,4096]{1,0:T(8,128)(2,1)}, bf16[64,4096]{1,0:T(8,128)(2,1)S(1)}, u32[]{:S(2)}) copy-start(bf16[64,4096]{1,0:T(8,128)(2,1)S(1)} %multiply_convert_fusion.3) | copy-start | bytes 1572868
  176.5 9.1 %copy-start.10 = (f32[2048]{0:T(1024)S(1)}, f32[2048]{0:T(1024)}, u32[]{:S(2)}) copy-start(f32[2048]{0:T(1024)} %param.33) | copy-start | bytes 24580
  194.4 98.4 %copy-start.14 = (bf16[1,2048,384]{2,1,0:T(8,128)(2,1)S(1)}, bf16[1,2048,384]{2,1,0:T(8,128)(2,1)}, u32[]{:S(2)}) copy-start(bf16[1,2048,384]{2,1,0:T(8,128)(2,1)} %param.37) | copy-start | bytes 4718596
  290.8 2.0 copy-start.1
  292.8 3.6 copy-start.15
  304.1 4.4 %copy-start.7 = (s32[64,10]{0,1:T(8,128)S(1)}, s32[64,10]{0,1:T(8,128)}, u32[]{:S(2)}) copy-start(s32[64,10]{0,1:T(8,128)} %param.35) | copy-start | bytes 7684
  304.1 97.7 %all-to-all-start.4 = ((bf16[32,32,2048]{2,1,0:T(8,128)(2,1)}), bf16[32,32,2048]{2,1,0:T(8,128)(2,1)}, u32[]{:S(2)}, u32[]{:S(2)}) async-start(bf16[32,32,2048]{2,1,0:T(8,128)(2,1)} %bitcast.88), calls=%async_computation.4 | async-start | bytes 8388608 | tf_op jit(solution)/shard_map/all_to_all | solution.py:143
Sparse Core Ops, SparseCore 0:
  10.8 151.8 all-gather.1
where the time goes:
time: 431 us; the launch traced here: 430 us
  blocking collectives  180 us (42%)
  waiting for transfers between devices  109 us (25%)
  local copies, waits for them, and re-layouts  55 us (13%)
  starting transfers between devices  30.1 us (7%)
  matrix products  26.2 us (6%)
  other arithmetic  15.2 us (4%)
  between operations  14.5 us (3%)
    all_to_all x1, blocking collectives, local(): lax.all_to_all(send_rows, 'wide', split_axis=0, concat_axis=0, tiled=True)  96.4 us
    all_to_all x1, waiting for transfers between devices, local(): lax.all_to_all(outputs, 'wide', split_axis=0, concat_axis=0, tiled=True)  93.2 us
    all_gather x1, blocking collectives, local(): c_all = lax.all_gather(ssd_c, 'wide', axis=0, tiled=True)  84.1 us
    all_to_all x1, starting transfers between devices, local(): lax.all_to_all(carried_head.reshape(tokens_all, per_dev * head_dim), 'wid...  15.3 us
    gather x2, local copies, waits for them, and re-layouts, local(): jnp.take(returned.reshape(devices * capacity, width), position, axis=0)  15.1 us
    all_to_all x1, waiting for transfers between devices, local(): lax.all_to_all(carried_head.reshape(tokens_all, per_dev * head_dim), 'wid...  10.9 us
    dot_general x1, matrix products, local(): jnp.dot(ssd_out, lax.all_gather(w_out, 'wide', axis=0, tiled=True), prefe...  9.07 us
  transfers between devices with their start and end apart: 5, of which 3 were waited for; matrix products, arithmetic and copies ran while one was open for 9% of the time, Pallas kernels for 0%

commit v1 on v0

--- a/solution.py
+++ b/solution.py
@@ -90,13 +90,10 @@
     head_raw = lax.all_to_all(dt_raw, "wide", split_axis=1, concat_axis=0, tiled=True)
     step_size, cumulative = head_steps(head_raw, bias_part, rate_part, requests)
     carried_head = state_terms(c_all.reshape(requests, SEQ, state_size), cumulative, start_state)
-    carried = lax.all_to_all(
-        carried_head.reshape(tokens_all, per_dev * head_dim),
-        "wide",
-        split_axis=0,
-        concat_axis=1,
-        tiled=True,
-    )
+    x = carried_head.reshape(tokens_all, per_dev * head_dim)
+    pieces = jnp.split(x, lax.axis_size("wide"), axis=0)
+    incoming = lax.all_to_all(jnp.stack(pieces), "wide", 0, 0)
+    carried = jnp.concatenate(incoming, axis=1)
     mixed = intra.astype(jnp.float32) + carried.astype(jnp.float32)
     gated = mixed * jax.nn.silu(ssd_z.astype(jnp.float32))
     ssd_out = (

time: 431 us -> 454 us (1.053)
  local copies, waits for them, and re-layouts: 55 us -> 77.4 us
    unnamed x40 -> x81, local copies, waits for them, and re-layouts: 6.61 us -> 26.4 us
    another operation x0 -> x33, local copies, waits for them, and re-layouts: none -> 5.94 us  [local(): incoming = lax.all_to_all(jnp.stack(pieces), 'wide', 0, 0)]
  transfers between devices with their start and end apart: 5 -> 5, of which waited for: 3 -> 3; matrix products, arithmetic and copies ran while one was open for 9% -> 14% of each run, Pallas kernels for 0% -> 0%
where the time goes in v1:
time: 454 us; the launch traced here: 453 us
  blocking collectives  180 us (40%)
  waiting for transfers between devices  109 us (24%)
  local copies, waits for them, and re-layouts  77.4 us (17%)
  starting transfers between devices  29.9 us (7%)
  matrix products  26.2 us (6%)
  other arithmetic  15.2 us (3%)
  between operations  14.8 us (3%)
    all_to_all x1, blocking collectives, local(): lax.all_to_all(send_rows, 'wide', split_axis=0, concat_axis=0, tiled=True)  96.4 us
    all_to_all x1, waiting for transfers between devices, local(): lax.all_to_all(outputs, 'wide', split_axis=0, concat_axis=0, tiled=True)  93.2 us
    all_gather x1, blocking collectives, local(): c_all = lax.all_gather(ssd_c, 'wide', axis=0, tiled=True)  84.1 us
    unnamed x81, local copies, waits for them, and re-layouts  26.4 us
    all_to_all x1, starting transfers between devices, local(): incoming = lax.all_to_all(jnp.stack(pieces), 'wide', 0, 0)  15.2 us
    gather x2, local copies, waits for them, and re-layouts, local(): jnp.take(returned.reshape(devices * capacity, width), position, axis=0)  15 us
    all_to_all x1, waiting for transfers between devices, local(): incoming = lax.all_to_all(jnp.stack(pieces), 'wide', 0, 0)  10.9 us
  transfers between devices with their start and end apart: 5, of which 3 were waited for; matrix products, arithmetic and copies ran while one was open for 14% of the time, Pallas kernels for 0%

profile of v1, /device:TPU:0, one launch (start us, length us, event | category | flops | bytes accessed | tf_op | source)
XLA Modules:
  0.0 452.6 jit_solution(13622627589758747923)
XLA Ops:
  7.2 0.7 all-gather.2.cloned.1.call-update
  7.9 1.4 copy.232
  9.3 7.3 %all-to-all-start.1 = ((bf16[64,32,2]{0,2,1:T(2,128)(2,1)}), bf16[64,32,2]{0,2,1:T(2,128)(2,1)S(1)}, u32[]{:S(2)}, u32[]{:S(2)}) async-start(bf16[64,32,2]{0,2,1:T(2,128)(2,1)} %bitcast.14), calls=%async_computation.1 | async-start | bytes 32768 | tf_op jit(solution)/shard_map/all_to_all | solution.py:90
  16.7 3.1 copy.229
  19.8 3.9 all-to-all-done.1
  23.8 3.5 all-to-all-start
  28.2 1.1 reshape.251
  29.5 1.9 fusion.12
  31.5 2.5 copy.228
  34.0 2.1 reshape.258
  36.2 1.5 reduce-window.6
  38.0 84.1 %all_gather.6 = bf16[2048,128]{1,0:T(8,128)(2,1)S(1)} all-gather(bf16[64,128]{1,0:T(8,128)(2,1)S(1)} %copy-done.11), channel_id=1, replica_groups=mesh['group'=1,'wide'=32] {'wide'}, dimensions={0}, use_global_device_ids=true | all-gather | bytes 540672 | tf_op jit(solution)/shard_map/all_gather | solution.py:89
  122.3 1.4 copy.235
  123.7 2.4 reduce-window_exponential_fusion
  126.1 1.9 copy.236
  127.9 3.2 copy.231
  131.1 3.7 gather_fusion
  134.9 3.7 fusion
  138.6 1.0 copy-done.3
  141.2 1.2 fusion.47
  142.4 0.7 stack.112
  143.2 0.7 stack.113
  143.9 0.7 stack.114
  144.7 0.7 stack.116
  147.2 0.6 constant_dynamic-update-slice_fusion.31
  147.8 0.6 constant_dynamic-update-slice_fusion.30
  148.4 0.6 constant_dynamic-update-slice_fusion.29
  149.0 0.6 constant_dynamic-update-slice_fusion.28
  149.6 0.6 constant_dynamic-update-slice_fusion.27
  150.2 0.6 constant_dynamic-update-slice_fusion.26
  150.8 0.6 constant_dynamic-update-slice_fusion.25
  151.4 0.6 constant_dynamic-update-slice_fusion.24
  153.3 0.6 constant_dynamic-update-slice_fusion.21
  153.9 0.6 constant_dynamic-update-slice_fusion.20
  154.5 0.6 constant_dynamic-update-slice_fusion.19
  155.1 0.6 constant_dynamic-update-slice_fusion.18
  155.7 0.6 constant_dynamic-update-slice_fusion.17
  156.3 0.6 constant_dynamic-update-slice_fusion.16
  156.9 0.6 constant_dynamic-update-slice_fusion.15
  157.5 0.6 constant_dynamic-update-slice_fusion.14
  158.1 0.6 constant_dynamic-update-slice_fusion.13
  158.7 0.6 constant_dynamic-update-slice_fusion.12
  159.3 0.6 constant_dynamic-update-slice_fusion.11
  161.2 0.6 constant_dynamic-update-slice_fusion.8
  161.8 0.6 constant_dynamic-update-slice_fusion.7
  162.4 0.6 constant_dynamic-update-slice_fusion.6
  163.0 0.6 constant_dynamic-update-slice_fusion.5
  163.6 0.6 constant_dynamic-update-slice_fusion.4
  166.6 15.2 %all-to-all-start.2 = ((bf16[32,64,128]{2,1,0:T(8,128)(2,1)}), bf16[32,64,128]{2,1,0:T(8,128)(2,1)S(1)}, u32[]{:S(2)}, u32[]{:S(2)}) async-start(bf16[32,64,128]{2,1,0:T(8,128)(2,1)} %constant_dynamic-update-slice_fusion), calls=%async_computation.2 | async-start | bytes 1048576 | tf_op jit(solution)/shard_map/all_to_all | solution.py:95
  182.2 4.1 scatter_custom_fusion
  186.5 10.9 %all-to-all-done.2 = bf16[32,64,128]{2,1,0:T(8,128)(2,1)S(1)} async-done(((bf16[32,64,128]{2,1,0:T(8,128)(2,1)}), bf16[32,64,128]{2,1,0:T(8,128)(2,1)S(1)}, u32[]{:S(2)}, u32[]{:S(2)}) %all-to-all-start.2) | async-done | bytes 524320 | tf_op jit(solution)/shard_map/all_to_all | solution.py:95
  197.5 1.5 multiply_reduce_fusion.1
  199.3 9.1 %multiply_reduce_fusion.2 = (f32[64]{0:T(128)S(1)}, f32[64,2048]{1,0:T(8,128)S(1)}) fusion(bf16[64,4096]{1,0:T(8,128)(2,1)S(1)} %multiply_convert_fusion.3, bf16[4096,2048]{1,0:T(8,128)(2,1)} %all-gather.2.cloned.1.call-done, bf16[64,2048]{1,0:T(8,128)(2,1)S(1)} %copy-done.5), kind=kOutput, calls=%fused_computation.42 | convolution fusion | flops 1074266112 | bytes 18088192 | tf_op jit(solution)/shard_map/dot_general | solution.py:103
  208.5 6.0 %gather_fusion.1 = bf16[1024,2048]{1,0:T(8,128)(2,1)} fusion(bf16[64,2048]{1,0:T(8,128)(2,1)S(1)} %multiply_convert_fusion.4, s32[1024]{0:T(1024)S(1)} %fusion.38), kind=kCustom, calls=%fused_computation.1 | custom fusion | bytes 8392704 | tf_op jit(solution)/shard_map/jit(_take)/gather | solution.py:133
  214.5 2.6 select_select_fusion
  217.0 96.4 %all_to_all.46 = bf16[32,32,2048]{2,1,0:T(8,128)(2,1)S(1)} all-to-all(bf16[32,32,2048]{2,1,0:T(8,128)(2,1)S(1)} %select_select_fusion), channel_id=1, replica_groups=mesh['group'=1,'wide'=32] {'wide'}, dimensions={0} | all-to-all | bytes 8388608 | tf_op jit(solution)/shard_map/all_to_all | solution.py:137
  313.4 2.0 copy-done.1
  315.4 3.6 fusion.8
  319.0 7.8 %convolution_convert_fusion = bf16[1024,2048]{1,0:T(8,128)(2,1)} fusion(bf16[1,384,2048]{2,1,0:T(8,128)(2,1)S(1)} %copy-done, f32[1024,384]{1,0:T(8,128)} %fusion.8, bf16[1024,2048]{1,0:T(8,128)(2,1)} %bitcast.90, bf16[1,2048,384]{2,1,0:T(8,128)(2,1)S(1)} %copy-done.20), kind=kOutput, calls=%fused_computation.6 | convolution fusion | flops 3225681920 | bytes 13107200 | tf_op jit(solution)/shard_map/dot_general | solution.py:33
  326.8 3.8 all-to-all-start.4
  331.1 93.2 %all-to-all-done.4 = bf16[32,32,2048]{2,1,0:T(8,128)(2,1)} async-done(((bf16[32,32,2048]{2,1,0:T(8,128)(2,1)}), bf16[32,32,2048]{2,1,0:T(8,128)(2,1)}, u32[]{:S(2)}, u32[]{:S(2)}) %all-to-all-start.4) | async-done | bytes 4194336 | tf_op jit(solution)/shard_map/all_to_all | solution.py:140
  424.3 9.7 %gather_fusion.2 = bf16[640,2048]{1,0:T(8,128)(2,1)} fusion(bf16[1024,2048]{1,0:T(8,128)(2,1)} %bitcast.24, s32[1024]{0:T(1024)S(1)} %pad_clamp_fusion), kind=kCustom, calls=%fused_computation.2 | custom fusion | bytes 5245440 | tf_op jit(solution)/shard_map/jit(_take)/gather | solution.py:141
  434.0 5.4 %gather.20 = bf16[64,10,2048]{2,1,0:T(8,128)(2,1)} reshape(bf16[640,2048]{1,0:T(8,128)(2,1)} %gather_fusion.2) | data formatting | bytes 5242880 | tf_op jit(solution)/shard_map/jit(_take)/gather | solution.py:141
  439.3 6.4 %multiply_reduce_fusion = bf16[64,2048]{1,0:T(8,128)(2,1)} fusion(f32[64,10]{1,0:T(8,128)S(1)} %copy.276, bf16[64,10,2048]{2,1,0:T(8,128)(2,1)} %gather.20, pred[64,10]{1,0:T(8,128)(4,1)S(1)} %copy.274), kind=kLoop, calls=%fused_computation.4 | loop fusion | flops 5111808 | bytes 2886784 | tf_op jit(solution)/shard_map/reduce_sum | solution.py:144
  (165 shorter events, 11.3 us)
Async XLA Ops:
  7.2 311.8 %copy-start = (bf16[1,384,2048]{2,1,0:T(8,128)(2,1)S(1)}, bf16[1,384,2048]{2,1,0:T(8,128)(2,1)}, u32[]{:S(2)}) copy-start(bf16[1,384,2048]{2,1,0:T(8,128)(2,1)} %param.39) | copy-start | bytes 4718596
  7.2 192.1 %all-gather.2.cloned.1.call-start = ((), (), s32[]{:S(2)}) async-start(), calls=%async_computation.5 | async-start | bytes 17301504 | tf_op jit(solution)/shard_map/all_gather | solution.py:105
  9.3 14.4 %all-to-all-start.1 = ((bf16[64,32,2]{0,2,1:T(2,128)(2,1)}), bf16[64,32,2]{0,2,1:T(2,128)(2,1)S(1)}, u32[]{:S(2)}, u32[]{:S(2)}) async-start(bf16[64,32,2]{0,2,1:T(2,128)(2,1)} %bitcast.14), calls=%async_computation.1 | async-start | bytes 32768 | tf_op jit(solution)/shard_map/all_to_all | solution.py:90
  19.8 7.5 %copy-start.16 = (s32[64,10]{0,1:T(8,128)S(1)}, s32[64,10]{0,1:T(8,128)}, u32[]{:S(2)}) copy-start(s32[64,10]{0,1:T(8,128)} %param.34) | copy-start | bytes 7684
  19.8 7.5 %copy-start.18 = (s32[32]{0:T(128)S(1)}, s32[32]{0:T(128)}, u32[]{:S(2)}) copy-start(s32[32]{0:T(128)} %param.36) | copy-start | bytes 388
  19.8 8.0 %copy-start.21 = (f32[64]{0:T(128)S(1)}, f32[64]{0:T(128)}, u32[]{:S(2)}) copy-start(f32[64]{0:T(128)} %param.26) | copy-start | bytes 772
  19.8 8.1 %copy-start.17 = (f32[64]{0:T(128)S(1)}, f32[64]{0:T(128)}, u32[]{:S(2)}) copy-start(f32[64]{0:T(128)} %param.25) | copy-start | bytes 772
  19.8 8.2 %copy-start.6 = (bf16[64,64]{1,0:T(8,128)(2,1)S(1)}, bf16[64,64]{1,0:T(8,128)(2,1)}, u32[]{:S(2)}) copy-start(bf16[64,64]{1,0:T(8,128)(2,1)} %param.24) | copy-start | bytes 24580
  19.8 8.4 %copy-start.4 = (bf16[64,4096]{1,0:T(8,128)(2,1)S(1)}, bf16[64,4096]{1,0:T(8,128)(2,1)}, u32[]{:S(2)}) copy-start(bf16[64,4096]{1,0:T(8,128)(2,1)} %param.20) | copy-start | bytes 1572868
  23.8 104.2 %all-to-all-start = ((bf16[2,64,64,128]{3,2,0,1:T(8,128)(2,1)}), bf16[2,64,64,128]{3,2,0,1:T(8,128)(2,1)}, u32[]{:S(2)}, u32[]{:S(2)}) async-start(bf16[2,64,64,128]{3,2,0,1:T(8,128)(2,1)} %copy.229), calls=%async_computation | async-start | bytes 4194304 | tf_op jit(solution)/shard_map/all_to_all | solution.py:75
  27.2 2.2 copy-start.11
  27.3 2.1 copy-start.14
  27.3 2.3 copy-start.22
  34.0 3.9 copy-start.23
  138.6 1.0 copy-start.3
  143.9 11.2 %copy-start.7 = (bf16[1,64,128]{2,1,0:T(8,128)(2,1)S(1)}, bf16[1,64,128]{2,1,0:T(8,128)(2,1)}, u32[]{:S(2)}) copy-start(bf16[1,64,128]{2,1,0:T(8,128)(2,1)} %stack.112) | copy-start | bytes 49156
  143.9 11.8 %copy-start.8 = (bf16[1,64,128]{2,1,0:T(8,128)(2,1)S(1)}, bf16[1,64,128]{2,1,0:T(8,128)(2,1)}, u32[]{:S(2)}) copy-start(bf16[1,64,128]{2,1,0:T(8,128)(2,1)} %stack.113) | copy-start | bytes 49156
  144.6 11.7 %copy-start.9 = (bf16[1,64,128]{2,1,0:T(8,128)(2,1)S(1)}, bf16[1,64,128]{2,1,0:T(8,128)(2,1)}, u32[]{:S(2)}) copy-start(bf16[1,64,128]{2,1,0:T(8,128)(2,1)} %stack.114) | copy-start | bytes 49156
  145.4 12.1 %copy-start.10 = (bf16[1,64,128]{2,1,0:T(8,128)(2,1)S(1)}, bf16[1,64,128]{2,1,0:T(8,128)(2,1)}, u32[]{:S(2)}) copy-start(bf16[1,64,128]{2,1,0:T(8,128)(2,1)} %stack.116) | copy-start | bytes 49156
  166.6 32.4 %copy-start.13 = (f32[4096]{0:T(1024)S(1)}, f32[4096]{0:T(1024)}, u32[]{:S(2)}) copy-start(f32[4096]{0:T(1024)} %param.28) | copy-start | bytes 49156
  166.6 30.8 %all-to-all-start.2 = ((bf16[32,64,128]{2,1,0:T(8,128)(2,1)}), bf16[32,64,128]{2,1,0:T(8,128)(2,1)S(1)}, u32[]{:S(2)}, u32[]{:S(2)}) async-start(bf16[32,64,128]{2,1,0:T(8,128)(2,1)} %constant_dynamic-update-slice_fusion), calls=%async_computation.2 | async-start | bytes 1048576 | tf_op jit(solution)/shard_map/all_to_all | solution.py:95
  186.5 12.7 %copy-start.5 = (bf16[64,2048]{1,0:T(8,128)(2,1)S(1)}, bf16[64,2048]{1,0:T(8,128)(2,1)}, u32[]{:S(2)}) copy-start(bf16[64,2048]{1,0:T(8,128)(2,1)} %param.31) | copy-start | bytes 786436
  199.2 9.1 %copy-start.2 = (bf16[64,4096]{1,0:T(8,128)(2,1)}, bf16[64,4096]{1,0:T(8,128)(2,1)S(1)}, u32[]{:S(2)}) copy-start(bf16[64,4096]{1,0:T(8,128)(2,1)S(1)} %multiply_convert_fusion.3) | copy-start | bytes 1572868
  199.2 9.1 %copy-start.15 = (f32[2048]{0:T(1024)S(1)}, f32[2048]{0:T(1024)}, u32[]{:S(2)}) copy-start(f32[2048]{0:T(1024)} %param.33) | copy-start | bytes 24580
  217.0 98.4 %copy-start.19 = (bf16[1,2048,384]{2,1,0:T(8,128)(2,1)S(1)}, bf16[1,2048,384]{2,1,0:T(8,128)(2,1)}, u32[]{:S(2)}) copy-start(bf16[1,2048,384]{2,1,0:T(8,128)(2,1)} %param.37) | copy-start | bytes 4718596
  313.4 2.0 copy-start.1
  315.4 3.6 copy-start.20
  326.8 4.1 copy-start.12
  326.8 97.5 %all-to-all-start.4 = ((bf16[32,32,2048]{2,1,0:T(8,128)(2,1)}), bf16[32,32,2048]{2,1,0:T(8,128)(2,1)}, u32[]{:S(2)}, u32[]{:S(2)}) async-start(bf16[32,32,2048]{2,1,0:T(8,128)(2,1)} %bitcast.88), calls=%async_computation.4 | async-start | bytes 8388608 | tf_op jit(solution)/shard_map/all_to_all | solution.py:140
Sparse Core Ops, SparseCore 0:
  10.8 151.8 all-gather.1
